TPU v7x, 32 devices: a whole 2x2x4 slice. The times are simulated.
32 devices in a mesh: rows: 8 (over z, y), cols: 4 (over x, core).
Axes of the slice: x: 2, y: 2, z: 4, core: 2. Of those that a mesh axis runs over, the one named last changes fastest.
Arguments:
- start_panel: float32 [64, 16384], P(None, ('rows', 'cols')), may hold values from -6 to 6
- tile_values: float32 [128, 16, 128, 128], P('rows', 'cols')
- tile_column: int32 [128, 16], P('rows', 'cols'), may hold values from 0 to 127, as said below
- tile_count: int32 [128], P('rows'), may hold values from 8 to 16, as said below
Outputs:
- basis: float32 [64, 16384], P(None, ('rows', 'cols'))
Inputs may be any that keep to these rules, and one draw needn't show every extreme that they name: `tile_count`: every row block has between half of its slots and all 16 slots live; some row block has all 16 live. `tile_column`: in row block i the entries are distinct column blocks, each within 16 blocks of i, and the first is i itself; slots at or beyond tile_count[i] hold such entries too but are not used.
All inputs are finite; a program needn't handle non-finite values.
Results may differ from a plain program's by a relative error of at most 0.0003.
Values sent between devices are 32-bit elements; how exact they have to be, the bound alone decides.
A program may use at most 64 MiB of HBM per device.

v0:
```python
import math

import jax
import jax.numpy as jnp
from jax import lax
from jax.sharding import PartitionSpec as P

ITERS = 3


def with_halo(block, sides, width):
    for axis, dim in sides:
        count = lax.axis_size(axis)
        forward = [(i, i + 1) for i in range(count - 1)]
        backward = [(target, source) for source, target in forward]
        low = lax.ppermute(
            lax.slice_in_dim(block, block.shape[dim] - width, None, axis=dim), axis, forward
        )
        high = lax.ppermute(lax.slice_in_dim(block, 0, width, axis=dim), axis, backward)
        block = jnp.concatenate([low, block, high], axis=dim)
    return block


def local_product(extended, tile_values, tile_column, tile_count):
    owned_blocks = tile_values.shape[0]
    slot_dev = tile_values.shape[1]
    tile_width = tile_values.shape[2]
    anchor = lax.axis_index("rows") * owned_blocks - owned_blocks
    local_column = tile_column - anchor
    blocks = extended.reshape(extended.shape[0], 3 * owned_blocks, tile_width)
    picked = jnp.take(blocks, local_column, axis=1)
    slot_ids = lax.axis_index("cols") * slot_dev + jnp.arange(slot_dev, dtype=jnp.int32)
    alive_mask = slot_ids[None, :] < tile_count[:, None]
    picked = jnp.where(alive_mask[None, :, :, None], picked, jnp.float32(0.0))
    result = jnp.einsum("disk,isnk->din", picked, tile_values, precision=lax.Precision.HIGHEST)
    return result.reshape(extended.shape[0], owned_blocks * tile_width)


def per_device(start_panel, tile_values, tile_column, tile_count):

    def fetch_owner(panel_part):
        return lax.all_gather(panel_part, "cols", axis=1, tiled=True)

    def partial_of(owner_panel):
        extended = with_halo(owner_panel, (("rows", 1),), owner_panel.shape[1])
        return local_product(extended, tile_values, tile_column, tile_count)

    def reduce_share(partial_terms):
        return lax.psum_scatter(partial_terms, "cols", scatter_dimension=1, tiled=True)

    panel = start_panel
    for sweep_index in range(ITERS):
        first_terms = partial_of(fetch_owner(panel))
        middle = fetch_owner(reduce_share(first_terms))
        second = reduce_share(partial_of(middle))
        local_gram = jnp.dot(
            second, second.T, precision=lax.Precision.HIGHEST, preferred_element_type=jnp.float32
        )
        lower_factor = jnp.linalg.cholesky(lax.psum(local_gram, ("rows", "cols")))
        panel = lax.linalg.triangular_solve(lower_factor, second, left_side=True, lower=True)
    scaling = math.sqrt(lax.axis_size("rows") * lax.axis_size("cols") * panel.shape[1])
    return panel * jnp.float32(scaling)


def solution(mesh):
    in_specs = (
        P(None, ("rows", "cols")),
        P("rows", "cols", None, None),
        P("rows", "cols"),
        P("rows"),
    )
    out_specs = P(None, ("rows", "cols"))
    return jax.shard_map(
        per_device, mesh=mesh, in_specs=in_specs, out_specs=out_specs, check_vma=False
    )
```

profile of v0, /device:TPU:0, one launch (start us, length us, event | category | flops | bytes accessed | tf_op | source)
XLA Modules:
  0.0 582.8 jit_solution(2102967249004942591)
XLA Ops:
  6.5 8.8 %all_gather.18 = f32[64,2048]{1,0:T(8,128)S(1)} all-gather(f32[64,512]{1,0:T(8,128)} %param.9), channel_id=1, replica_groups=mesh['rows'=8,'cols'=4] {'cols'}, dimensions={1}, use_global_device_ids=true | all-gather | bytes 655360 | tf_op jit(solution)/shard_map/all_gather | solution.py:42
  23.0 8.5 %collective-permute-done.1 = f32[64,2048]{1,0:T(8,128)S(1)} collective-permute-done((f32[64,2048]{1,0:T(8,128)S(1)}, f32[64,2048]{1,0:T(8,128)S(1)}, u32[]{:S(2)}, u32[]{:S(2)}) %collective-permute-start.1) | collective-permute-done | bytes 524320 | tf_op jit(solution)/shard_map/ppermute | solution.py:19
  31.4 11.2 %collective-permute-done = f32[64,2048]{1,0:T(8,128)S(1)} collective-permute-done((f32[64,2048]{1,0:T(8,128)S(1)}, f32[64,2048]{1,0:T(8,128)S(1)}, u32[]{:S(2)}, u32[]{:S(2)}) %collective-permute-start) | collective-permute-done | bytes 524320 | tf_op jit(solution)/shard_map/ppermute | solution.py:16
  53.2 22.6 %reduce-scatter.7.cloned.1.call-done = f32[64,512]{1,0:T(8,128)} async-done(((f32[64,2048]{1,0:T(8,128)}), f32[64,512]{1,0:T(8,128)}) %reduce-scatter.7.cloned.1.call-update) | async-done | bytes 131088 | tf_op jit(solution)/shard_map/reduce_scatter | solution.py:49
  88.6 10.2 %collective-permute-done.3 = f32[64,2048]{1,0:T(8,128)S(1)} collective-permute-done((f32[64,2048]{1,0:T(8,128)S(1)}, f32[64,2048]{1,0:T(8,128)S(1)}, u32[]{:S(2)}, u32[]{:S(2)}) %collective-permute-start.3) | collective-permute-done | bytes 524320 | tf_op jit(solution)/shard_map/ppermute | solution.py:19
  98.8 11.1 %collective-permute-done.2 = f32[64,2048]{1,0:T(8,128)S(1)} collective-permute-done((f32[64,2048]{1,0:T(8,128)S(1)}, f32[64,2048]{1,0:T(8,128)S(1)}, u32[]{:S(2)}, u32[]{:S(2)}) %collective-permute-start.2) | collective-permute-done | bytes 524320 | tf_op jit(solution)/shard_map/ppermute | solution.py:16
  120.5 22.2 %reduce-scatter.9.cloned.1.call-done = f32[64,512]{1,0:T(8,128)} async-done(((f32[64,2048]{1,0:T(8,128)}), f32[64,512]{1,0:T(8,128)}) %reduce-scatter.9.cloned.1.call-update) | async-done | bytes 131088 | tf_op jit(solution)/shard_map/reduce_scatter | solution.py:49
  143.9 39.7 %psum.21 = f32[64,64]{0,1:T(8,128)S(1)} all-reduce(f32[64,64]{0,1:T(8,128)S(1)} %fusion.69), channel_id=1, replica_groups=mesh['rows'=8,'cols'=4] {'rows','cols'}, use_global_device_ids=true, to_apply=%region_2.4 | all-reduce | flops 4096 | bytes 32768 | tf_op jit(solution)/shard_map/psum | solution.py:59
  197.0 7.9 %all_gather.20 = f32[64,2048]{1,0:T(8,128)S(1)} all-gather(f32[64,512]{1,0:T(8,128)S(1)} %fusion.50), channel_id=1, replica_groups=mesh['rows'=8,'cols'=4] {'cols'}, dimensions={1}, use_global_device_ids=true | all-gather | bytes 655360 | tf_op jit(solution)/shard_map/all_gather | solution.py:42
  210.8 10.2 %collective-permute-done.5 = f32[64,2048]{1,0:T(8,128)S(1)} collective-permute-done((f32[64,2048]{1,0:T(8,128)S(1)}, f32[64,2048]{1,0:T(8,128)S(1)}, u32[]{:S(2)}, u32[]{:S(2)}) %collective-permute-start.5) | collective-permute-done | bytes 524320 | tf_op jit(solution)/shard_map/ppermute | solution.py:19
  221.0 11.2 %collective-permute-done.4 = f32[64,2048]{1,0:T(8,128)S(1)} collective-permute-done((f32[64,2048]{1,0:T(8,128)S(1)}, f32[64,2048]{1,0:T(8,128)S(1)}, u32[]{:S(2)}, u32[]{:S(2)}) %collective-permute-start.4) | collective-permute-done | bytes 524320 | tf_op jit(solution)/shard_map/ppermute | solution.py:16
  242.7 22.1 %reduce-scatter.11.cloned.1.call-done = f32[64,512]{1,0:T(8,128)} async-done(((f32[64,2048]{1,0:T(8,128)}), f32[64,512]{1,0:T(8,128)}) %reduce-scatter.11.cloned.1.call-update) | async-done | bytes 131088 | tf_op jit(solution)/shard_map/reduce_scatter | solution.py:49
  277.7 10.2 %collective-permute-done.7 = f32[64,2048]{1,0:T(8,128)S(1)} collective-permute-done((f32[64,2048]{1,0:T(8,128)S(1)}, f32[64,2048]{1,0:T(8,128)S(1)}, u32[]{:S(2)}, u32[]{:S(2)}) %collective-permute-start.7) | collective-permute-done | bytes 524320 | tf_op jit(solution)/shard_map/ppermute | solution.py:19
  287.9 11.1 %collective-permute-done.6 = f32[64,2048]{1,0:T(8,128)S(1)} collective-permute-done((f32[64,2048]{1,0:T(8,128)S(1)}, f32[64,2048]{1,0:T(8,128)S(1)}, u32[]{:S(2)}, u32[]{:S(2)}) %collective-permute-start.6) | collective-permute-done | bytes 524320 | tf_op jit(solution)/shard_map/ppermute | solution.py:16
  309.6 22.2 %reduce-scatter.13.cloned.1.call-done = f32[64,512]{1,0:T(8,128)} async-done(((f32[64,2048]{1,0:T(8,128)}), f32[64,512]{1,0:T(8,128)}) %reduce-scatter.13.cloned.1.call-update) | async-done | bytes 131088 | tf_op jit(solution)/shard_map/reduce_scatter | solution.py:49
  333.0 39.7 %psum.22 = f32[64,64]{0,1:T(8,128)S(1)} all-reduce(f32[64,64]{0,1:T(8,128)S(1)} %fusion.70), channel_id=1, replica_groups=mesh['rows'=8,'cols'=4] {'rows','cols'}, use_global_device_ids=true, to_apply=%region_7.11 | all-reduce | flops 4096 | bytes 32768 | tf_op jit(solution)/shard_map/psum | solution.py:59
  386.1 7.9 %all_gather.22 = f32[64,2048]{1,0:T(8,128)S(1)} all-gather(f32[64,512]{1,0:T(8,128)S(1)} %fusion.47), channel_id=1, replica_groups=mesh['rows'=8,'cols'=4] {'cols'}, dimensions={1}, use_global_device_ids=true | all-gather | bytes 655360 | tf_op jit(solution)/shard_map/all_gather | solution.py:42
  400.0 10.2 %collective-permute-done.9 = f32[64,2048]{1,0:T(8,128)S(1)} collective-permute-done((f32[64,2048]{1,0:T(8,128)S(1)}, f32[64,2048]{1,0:T(8,128)S(1)}, u32[]{:S(2)}, u32[]{:S(2)}) %collective-permute-start.9) | collective-permute-done | bytes 524320 | tf_op jit(solution)/shard_map/ppermute | solution.py:19
  410.1 11.2 %collective-permute-done.8 = f32[64,2048]{1,0:T(8,128)S(1)} collective-permute-done((f32[64,2048]{1,0:T(8,128)S(1)}, f32[64,2048]{1,0:T(8,128)S(1)}, u32[]{:S(2)}, u32[]{:S(2)}) %collective-permute-start.8) | collective-permute-done | bytes 524320 | tf_op jit(solution)/shard_map/ppermute | solution.py:16
  431.9 22.0 %reduce-scatter.15.cloned.1.call-done = f32[64,512]{1,0:T(8,128)} async-done(((f32[64,2048]{1,0:T(8,128)}), f32[64,512]{1,0:T(8,128)}) %reduce-scatter.15.cloned.1.call-update) | async-done | bytes 131088 | tf_op jit(solution)/shard_map/reduce_scatter | solution.py:49
  466.8 10.2 %collective-permute-done.11 = f32[64,2048]{1,0:T(8,128)S(1)} collective-permute-done((f32[64,2048]{1,0:T(8,128)S(1)}, f32[64,2048]{1,0:T(8,128)S(1)}, u32[]{:S(2)}, u32[]{:S(2)}) %collective-permute-start.11) | collective-permute-done | bytes 524320 | tf_op jit(solution)/shard_map/ppermute | solution.py:19
  477.0 11.1 %collective-permute-done.10 = f32[64,2048]{1,0:T(8,128)S(1)} collective-permute-done((f32[64,2048]{1,0:T(8,128)S(1)}, f32[64,2048]{1,0:T(8,128)S(1)}, u32[]{:S(2)}, u32[]{:S(2)}) %collective-permute-start.10) | collective-permute-done | bytes 524320 | tf_op jit(solution)/shard_map/ppermute | solution.py:16
  498.6 22.3 %reduce-scatter.17.cloned.1.call-done = f32[64,512]{1,0:T(8,128)} async-done(((f32[64,2048]{1,0:T(8,128)}), f32[64,512]{1,0:T(8,128)}) %reduce-scatter.17.cloned.1.call-update) | async-done | bytes 131088 | tf_op jit(solution)/shard_map/reduce_scatter | solution.py:49
  522.1 39.8 %psum.23 = f32[64,64]{0,1:T(8,128)S(1)} all-reduce(f32[64,64]{0,1:T(8,128)S(1)} %fusion.71), channel_id=1, replica_groups=mesh['rows'=8,'cols'=4] {'rows','cols'}, use_global_device_ids=true, to_apply=%region_10.14 | all-reduce | flops 4096 | bytes 32768 | tf_op jit(solution)/shard_map/psum | solution.py:59
  (85 shorter events, 165.6 us)
Async XLA Ops:
  6.5 69.2 %reduce-scatter.7.cloned.1.call-start = ((), (), s32[]{:S(2)}) async-start(), calls=%async_computation.6 | async-start | bytes 655360 | tf_op jit(solution)/shard_map/reduce_scatter | solution.py:49
  15.4 16.1 %collective-permute-start.1 = (f32[64,2048]{1,0:T(8,128)S(1)}, f32[64,2048]{1,0:T(8,128)S(1)}, u32[]{:S(2)}, u32[]{:S(2)}) collective-permute-start(f32[64,2048]{1,0:T(8,128)S(1)} %all_gather.18), channel_id=1, source_target_pairs={{4,0},{8,4},{12,8},{16,12},{20,16},{24,20},{28,24},{5,1},{9,5},{13... | collective-permute-start | bytes 1572872 | tf_op jit(solution)/shard_map/ppermute | solution.py:19
  16.6 25.9 %collective-permute-start = (f32[64,2048]{1,0:T(8,128)S(1)}, f32[64,2048]{1,0:T(8,128)S(1)}, u32[]{:S(2)}, u32[]{:S(2)}) collective-permute-start(f32[64,2048]{1,0:T(8,128)S(1)} %all_gather.18), channel_id=1, source_target_pairs={{0,4},{4,8},{8,12},{12,16},{16,20},{20,24},{24,28},{1,5},{5,9},{9,... | collective-permute-start | bytes 1572872 | tf_op jit(solution)/shard_map/ppermute | solution.py:16
  53.1 89.5 %reduce-scatter.9.cloned.1.call-start = ((), (), s32[]{:S(2)}) async-start(), calls=%async_computation.7 | async-start | bytes 655360 | tf_op jit(solution)/shard_map/reduce_scatter | solution.py:49
  82.7 16.1 %collective-permute-start.3 = (f32[64,2048]{1,0:T(8,128)S(1)}, f32[64,2048]{1,0:T(8,128)S(1)}, u32[]{:S(2)}, u32[]{:S(2)}) collective-permute-start(f32[64,2048]{1,0:T(8,128)S(1)} %all_gather.19), channel_id=1, source_target_pairs={{4,0},{8,4},{12,8},{16,12},{20,16},{24,20},{28,24},{5,1},{9,5},{13... | collective-permute-start | bytes 1572872 | tf_op jit(solution)/shard_map/ppermute | solution.py:19
  84.0 25.9 %collective-permute-start.2 = (f32[64,2048]{1,0:T(8,128)S(1)}, f32[64,2048]{1,0:T(8,128)S(1)}, u32[]{:S(2)}, u32[]{:S(2)}) collective-permute-start(f32[64,2048]{1,0:T(8,128)S(1)} %all_gather.19), channel_id=1, source_target_pairs={{0,4},{4,8},{8,12},{12,16},{16,20},{20,24},{24,28},{1,5},{5,9},{9,... | collective-permute-start | bytes 1572872 | tf_op jit(solution)/shard_map/ppermute | solution.py:16
  120.4 144.4 %reduce-scatter.11.cloned.1.call-start = ((), (), s32[]{:S(2)}) async-start(), calls=%async_computation.8 | async-start | bytes 655360 | tf_op jit(solution)/shard_map/reduce_scatter | solution.py:49
  204.9 16.1 %collective-permute-start.5 = (f32[64,2048]{1,0:T(8,128)S(1)}, f32[64,2048]{1,0:T(8,128)S(1)}, u32[]{:S(2)}, u32[]{:S(2)}) collective-permute-start(f32[64,2048]{1,0:T(8,128)S(1)} %all_gather.20), channel_id=1, source_target_pairs={{4,0},{8,4},{12,8},{16,12},{20,16},{24,20},{28,24},{5,1},{9,5},{13... | collective-permute-start | bytes 1572872 | tf_op jit(solution)/shard_map/ppermute | solution.py:19
  206.2 25.9 %collective-permute-start.4 = (f32[64,2048]{1,0:T(8,128)S(1)}, f32[64,2048]{1,0:T(8,128)S(1)}, u32[]{:S(2)}, u32[]{:S(2)}) collective-permute-start(f32[64,2048]{1,0:T(8,128)S(1)} %all_gather.20), channel_id=1, source_target_pairs={{0,4},{4,8},{8,12},{12,16},{16,20},{20,24},{24,28},{1,5},{5,9},{9,... | collective-permute-start | bytes 1572872 | tf_op jit(solution)/shard_map/ppermute | solution.py:16
  242.7 89.1 %reduce-scatter.13.cloned.1.call-start = ((), (), s32[]{:S(2)}) async-start(), calls=%async_computation.9 | async-start | bytes 655360 | tf_op jit(solution)/shard_map/reduce_scatter | solution.py:49
  271.8 16.1 %collective-permute-start.7 = (f32[64,2048]{1,0:T(8,128)S(1)}, f32[64,2048]{1,0:T(8,128)S(1)}, u32[]{:S(2)}, u32[]{:S(2)}) collective-permute-start(f32[64,2048]{1,0:T(8,128)S(1)} %all_gather.21), channel_id=1, source_target_pairs={{4,0},{8,4},{12,8},{16,12},{20,16},{24,20},{28,24},{5,1},{9,5},{13... | collective-permute-start | bytes 1572872 | tf_op jit(solution)/shard_map/ppermute | solution.py:19
  273.1 25.9 %collective-permute-start.6 = (f32[64,2048]{1,0:T(8,128)S(1)}, f32[64,2048]{1,0:T(8,128)S(1)}, u32[]{:S(2)}, u32[]{:S(2)}) collective-permute-start(f32[64,2048]{1,0:T(8,128)S(1)} %all_gather.21), channel_id=1, source_target_pairs={{0,4},{4,8},{8,12},{12,16},{16,20},{20,24},{24,28},{1,5},{5,9},{9,... | collective-permute-start | bytes 1572872 | tf_op jit(solution)/shard_map/ppermute | solution.py:16
  309.5 144.4 %reduce-scatter.15.cloned.1.call-start = ((), (), s32[]{:S(2)}) async-start(), calls=%async_computation.10 | async-start | bytes 655360 | tf_op jit(solution)/shard_map/reduce_scatter | solution.py:49
  394.1 16.1 %collective-permute-start.9 = (f32[64,2048]{1,0:T(8,128)S(1)}, f32[64,2048]{1,0:T(8,128)S(1)}, u32[]{:S(2)}, u32[]{:S(2)}) collective-permute-start(f32[64,2048]{1,0:T(8,128)S(1)} %all_gather.22), channel_id=1, source_target_pairs={{4,0},{8,4},{12,8},{16,12},{20,16},{24,20},{28,24},{5,1},{9,5},{13... | collective-permute-start | bytes 1572872 | tf_op jit(solution)/shard_map/ppermute | solution.py:19
  395.4 26.0 %collective-permute-start.8 = (f32[64,2048]{1,0:T(8,128)S(1)}, f32[64,2048]{1,0:T(8,128)S(1)}, u32[]{:S(2)}, u32[]{:S(2)}) collective-permute-start(f32[64,2048]{1,0:T(8,128)S(1)} %all_gather.22), channel_id=1, source_target_pairs={{0,4},{4,8},{8,12},{12,16},{16,20},{20,24},{24,28},{1,5},{5,9},{9,... | collective-permute-start | bytes 1572872 | tf_op jit(solution)/shard_map/ppermute | solution.py:16
  431.9 89.0 %reduce-scatter.17.cloned.1.call-start = ((), (), s32[]{:S(2)}) async-start(), calls=%async_computation.11 | async-start | bytes 655360 | tf_op jit(solution)/shard_map/reduce_scatter | solution.py:49
  460.9 16.1 %collective-permute-start.11 = (f32[64,2048]{1,0:T(8,128)S(1)}, f32[64,2048]{1,0:T(8,128)S(1)}, u32[]{:S(2)}, u32[]{:S(2)}) collective-permute-start(f32[64,2048]{1,0:T(8,128)S(1)} %all_gather.23), channel_id=1, source_target_pairs={{4,0},{8,4},{12,8},{16,12},{20,16},{24,20},{28,24},{5,1},{9,5},{13... | collective-permute-start | bytes 1572872 | tf_op jit(solution)/shard_map/ppermute | solution.py:19
  462.2 25.9 %collective-permute-start.10 = (f32[64,2048]{1,0:T(8,128)S(1)}, f32[64,2048]{1,0:T(8,128)S(1)}, u32[]{:S(2)}, u32[]{:S(2)}) collective-permute-start(f32[64,2048]{1,0:T(8,128)S(1)} %all_gather.23), channel_id=1, source_target_pairs={{0,4},{4,8},{8,12},{12,16},{16,20},{20,24},{24,28},{1,5},{5,9},{9,... | collective-permute-start | bytes 1572872 | tf_op jit(solution)/shard_map/ppermute | solution.py:16
Sparse Core Ops, SparseCore 0:
  53.2 22.4 reduce-scatter.6
  120.5 22.0 reduce-scatter.8
  242.8 21.9 reduce-scatter.10
  309.6 22.0 reduce-scatter.12
  432.0 21.9 reduce-scatter.14
  498.7 22.0 reduce-scatter.16
where the time goes:
time: 584 us; the launch traced here: 583 us
  waiting for transfers between devices  260 us (45%)
  blocking collectives  165 us (28%)
  matrix products  52.7 us (9%)
  other arithmetic  38.8 us (7%)
  starting transfers between devices  35.4 us (6%)
  local copies, waits for them, and re-layouts  17.7 us (3%)
  between operations  13.8 us (2%)
    reduce_scatter x6, waiting for transfers between devices, reduce_share(): lax.psum_scatter(partial_terms, 'cols', scatter_dimension=1, tiled=True)  133 us
    psum x3, blocking collectives, per_device(): lower_factor = jnp.linalg.cholesky(lax.psum(local_gram, ('rows', 'cols')))  119 us
    ppermute x6, waiting for transfers between devices, with_halo(): lax.ppermute(lax.slice_in_dim(block, block.shape[dim] - width, None, axis...  66.9 us
    ppermute x6, waiting for transfers between devices, with_halo(): lax.ppermute(lax.slice_in_dim(block, 0, width, axis=dim), axis, backward)  59.4 us
    all_gather x6, blocking collectives, fetch_owner(): return lax.all_gather(panel_part, 'cols', axis=1, tiled=True)  45.6 us
    dot_general x6, matrix products, local_product(): jnp.einsum('disk,isnk->din', picked, tile_values, precision=lax.Precision...  44.6 us
    ppermute x6, starting transfers between devices, with_halo(): lax.ppermute(lax.slice_in_dim(block, block.shape[dim] - width, None, axis...  27.5 us
    another operation x9, other arithmetic, per_device(): lower_factor = jnp.linalg.cholesky(lax.psum(local_gram, ('rows', 'cols')))  19.6 us
  transfers between devices with their start and end apart: 18, of which 18 were waited for; matrix products, arithmetic and copies ran while one was open for 0% of the time, Pallas kernels for 0%

commit v1 on v0

v1 whole, which is shorter than its diff:
```python
import functools
import math

import jax
import jax.numpy as jnp
from jax import lax
from jax.experimental import pallas as pl
from jax.experimental.pallas import tpu as pltpu
from jax.sharding import PartitionSpec as P

ITERS = 3
HIGHEST = lax.Precision.HIGHEST
F32 = jnp.float32
BF16 = jnp.bfloat16

GATHER, LOW, HIGH, LOW_X, HIGH_X, REDUCE, SPREAD, PAIR = range(8)
KINDS = 8


def inverse_factor(gram):
    size = gram.shape[0]
    rows = lax.broadcasted_iota(jnp.int32, (size, size), 0)
    lanes = lax.broadcasted_iota(jnp.int32, (size, size), 1)
    both = jnp.concatenate([gram, jnp.where(rows == lanes, 1.0, 0.0).astype(F32)], axis=1)
    row_ids = lax.broadcasted_iota(jnp.int32, (size, 1), 0)
    scale = jnp.ones((size, 1), F32)
    for j in range(size):
        column = both[:, j : j + 1]
        row = both[j : j + 1, :]
        pivot = both[j : j + 1, j : j + 1]
        factor = jnp.where(row_ids > j, column / pivot, 0.0)
        scale = jnp.where(row_ids == j, lax.rsqrt(pivot), scale)
        both = both - factor * row
    return both[:, size:] * scale


def kernel(
    n_rows, start_ref, tiles_ref, slots_ref, out_ref,
    ext, planes, part, reduced, summed, share, pair, own_tiles, mate_tiles, t_hi, t_lo,
    mate_slots, own_index, mate_index, weight, gram_send, gram_recv,
    send_sem, recv_sem, gram_send_sem, gram_recv_sem, tile_sem, tile_send_sem, tile_recv_sem,
    slot_sem,
):
    r = lax.axis_index("rows")
    c = lax.axis_index("cols")
    half = c // 2
    mode = c % 2
    modes = ext.shape[2]
    owned = part.shape[0]
    hb = owned // 2
    qb = owned // 4
    slot_dev = own_tiles.shape[1]
    width = part.shape[2]
    other_half = c + 2 - 4 * half
    mate = c + 1 - 2 * mode
    row_rounds = int(math.log2(n_rows))

    def xor_rows(b):
        step = 1 << b
        bit = (r // step) % 2
        return r + step - 2 * step * bit

    gram_partners = [{"cols": mate}, {"cols": other_half}]
    gram_partners += [{"rows": xor_rows(b)} for b in range(row_rounds)]

    barrier = pltpu.get_barrier_semaphore()
    for partner in gram_partners:
        pl.semaphore_signal(barrier, inc=1, device_id=partner, device_id_type=pl.DeviceIdType.MESH)
    has_low = r > 0
    has_high = r < n_rows - 1

    @pl.when(has_low)
    def _():
        pl.semaphore_signal(barrier, inc=1, device_id={"rows": r - 1}, device_id_type=pl.DeviceIdType.MESH)

    @pl.when(has_high)
    def _():
        pl.semaphore_signal(barrier, inc=1, device_id={"rows": r + 1}, device_id_type=pl.DeviceIdType.MESH)

    edges = jnp.where(r == 0, 1, 0) + jnp.where(r == n_rows - 1, 1, 0)
    pl.semaphore_wait(barrier, len(gram_partners) + 2 - edges)

    def remote(src, dst, t, kind, device):
        return pltpu.make_async_remote_copy(
            src_ref=src, dst_ref=dst, send_sem=send_sem.at[t, kind], recv_sem=recv_sem.at[t, kind],
            device_id=device, device_id_type=pl.DeviceIdType.MESH,
        )

    def span(t, owner, piece_half):
        return ext.at[t, pl.ds(owner * owned + piece_half * hb, hb)]

    def gather_copy(t):
        return remote(span(t, 1, half), span(t, 1, half), t, GATHER, {"cols": other_half})

    def up_copy(t):
        return remote(span(t, 1, half), span(t, 0, half), t, LOW, {"rows": r + 1})

    def down_copy(t):
        return remote(span(t, 1, half), span(t, 2, half), t, HIGH, {"rows": r - 1})

    def low_forward(t):
        return remote(span(t, 0, half), span(t, 0, half), t, LOW_X, {"cols": other_half})

    def high_forward(t):
        return remote(span(t, 2, half), span(t, 2, half), t, HIGH_X, {"cols": other_half})

    def reduce_copy(t):
        return remote(part.at[pl.ds((1 - half) * hb, hb)], reduced.at[t], t, REDUCE, {"cols": other_half})

    def spread_copy(t):
        place = ext.at[t, pl.ds(owned + half * hb + mode * qb, qb)]
        return remote(share.at[1 - mode], place, t, SPREAD, {"cols": mate})

    def pair_copy(k):
        src = summed.at[k, pl.ds((1 - mode) * qb, qb)]
        return remote(src, pair.at[k], 2 * k + 1, PAIR, {"cols": mate})

    def send_halo(t):
        @pl.when(has_high)
        def _():
            up_copy(t).start()

        @pl.when(has_low)
        def _():
            down_copy(t).start()

        gather_copy(t).start()

    def forward_halo(t):
        @pl.when(has_low)
        def _():
            up_copy(t).wait_recv()
            low_forward(t).start()

        @pl.when(has_high)
        def _():
            down_copy(t).wait_recv()
            high_forward(t).start()

    def finish_halo(t):
        gather_copy(t).wait()

        @pl.when(has_low)
        def _():
            low_forward(t).wait()
            down_copy(t).wait_send()

        @pl.when(has_high)
        def _():
            high_forward(t).wait()
            up_copy(t).wait_send()

    def start_spread(t):
        spread_copy(t).start()
        for b in range(qb):
            ext[t, owned + half * hb + mode * qb + b] = share[mode, b]

    def finish_spread(t):
        spread_copy(t).wait()

    tile_parts = tile_sem.shape[0]
    per = owned // tile_parts

    def tile_local(q):
        rows = pl.ds(q * per, per)
        return pltpu.make_async_copy(tiles_ref.at[rows], own_tiles.at[rows], tile_sem.at[q])

    def tile_remote(q):
        rows = pl.ds(q * per, per)
        return pltpu.make_async_remote_copy(
            src_ref=tiles_ref.at[rows], dst_ref=mate_tiles.at[rows], send_sem=tile_send_sem.at[q],
            recv_sem=tile_recv_sem.at[q], device_id={"cols": mate}, device_id_type=pl.DeviceIdType.MESH,
        )

    slot_remote = pltpu.make_async_remote_copy(
        src_ref=slots_ref, dst_ref=mate_slots, send_sem=slot_sem.at[0], recv_sem=slot_sem.at[1],
        device_id={"cols": mate}, device_id_type=pl.DeviceIdType.MESH,
    )
    slot_remote.start()
    for b in range(qb):
        for h in range(2):
            share[h, b] = start_ref[h * modes : (h + 1) * modes, b * width : (b + 1) * width]
    start_spread(0)
    for q in range(tile_parts):
        tile_local(q).start()
        tile_remote(q).start()
    slot_own = pltpu.make_async_copy(slots_ref, own_index, slot_sem.at[2])
    slot_own.start()
    finish_spread(0)
    send_halo(0)
    slot_remote.wait()
    slot_mate = pltpu.make_async_copy(mate_slots, mate_index, slot_sem.at[3])
    slot_mate.start()
    slot_own.wait()
    slot_mate.wait()

    def split_tiles(source, q, offset):
        def body(i, carry):
            for s in range(slot_dev):
                tile = source[i, s]
                high = tile.astype(BF16)
                lanes = slice((offset + s) * width, (offset + s + 1) * width)
                t_hi[i, :, lanes] = high
                t_lo[i, :, lanes] = (tile - high.astype(F32)).astype(BF16)
            return carry

        lax.fori_loop(q * per, (q + 1) * per, body, 0)

    for q in range(tile_parts):
        tile_local(q).wait()
        split_tiles(own_tiles, q, 0)
    forward_halo(0)
    for q in range(tile_parts):
        tile_remote(q).wait()
        split_tiles(mate_tiles, q, slot_dev)

    weight_rows = lax.broadcasted_iota(jnp.int32, weight.shape, 0)
    weight_lanes = lax.broadcasted_iota(jnp.int32, weight.shape, 1)
    weight[...] = jnp.where(weight_rows == weight_lanes, 1.0, 0.0).astype(F32)
    blocks = 3 * owned
    planes[blocks] = jnp.zeros(planes.shape[1:], BF16)

    def row_product(i):
        picks = [planes[own_index[i, s]] for s in range(slot_dev)]
        picks += [planes[mate_index[i, s]] for s in range(slot_dev)]
        left = jnp.concatenate(picks, axis=1)
        contract = (((1,), (1,)), ((), ()))
        main = lax.dot_general(left, t_hi[i], contract, preferred_element_type=F32)
        rest = lax.dot_general(left[:modes], t_lo[i], contract, preferred_element_type=F32)
        part[i] = main[:modes] + (main[modes:] + rest)

    def apply(t):
        def convert(b, carry):
            value = ext[t, b]
            high = value.astype(BF16)
            planes[b, :modes] = high
            planes[b, modes:] = (value - high.astype(F32)).astype(BF16)
            return carry

        lax.fori_loop(0, blocks, convert, 0, unroll=4)

        def product(i, carry):
            row_product((1 - half) * hb + i)
            return carry

        lax.fori_loop(0, hb, product, 0, unroll=2)
        reduce_copy(t).start()

        def product_own(i, carry):
            row_product(half * hb + i)
            return carry

        lax.fori_loop(0, hb, product_own, 0, unroll=2)
        reduce_copy(t).wait()

    def add_reduced(t, target):
        def body(b, carry):
            ext[target, owned + half * hb + b] = part[half * hb + b] + reduced[t, b]
            return carry

        lax.fori_loop(0, hb, body, 0)

    def gram_round(k, b):
        copy = pltpu.make_async_remote_copy(
            src_ref=gram_send.at[k, b], dst_ref=gram_recv.at[k, b], send_sem=gram_send_sem.at[k, b],
            recv_sem=gram_recv_sem.at[k, b], device_id=gram_partners[b], device_id_type=pl.DeviceIdType.MESH,
        )
        return copy

    rounds = len(gram_partners)

    def sum_round(k, b):
        gram_round(k, b).wait()
        total = gram_send[k, b] + gram_recv[k, b]
        if b + 1 < rounds:
            gram_send[k, b + 1] = total
            gram_round(k, b + 1).start()
        return total

    def sweep(k, carry):
        t = 2 * k
        finish_halo(t)
        apply(t)
        add_reduced(t, t + 1)
        send_halo(t + 1)
        forward_halo(t + 1)
        finish_halo(t + 1)
        apply(t + 1)
        def close(b, carry):
            summed[k, b] = part[half * hb + b] + reduced[t + 1, b]
            return carry

        lax.fori_loop(0, hb, close, 0)
        pair_copy(k).start()
        for b in range(qb):
            share[mode, b] = summed[k, mode * qb + b]
        pair_copy(k).wait()
        for b in range(qb):
            share[1 - mode, b] = pair[k, b]
        raw = jnp.concatenate(
            [jnp.concatenate([share[0, b], share[1, b]], axis=0) for b in range(qb)], axis=1
        )
        mixed = jnp.dot(weight[...], raw, precision=HIGHEST, preferred_element_type=F32)
        for b in range(qb):
            for h in range(2):
                share[h, b] = mixed[h * modes : (h + 1) * modes, b * width : (b + 1) * width]
        gram_send[k, 0] = lax.dot_general(
            mixed, mixed, (((1,), (1,)), ((), ())), precision=HIGHEST, preferred_element_type=F32
        )
        gram_round(k, 0).start()

        more = k < ITERS - 1

        @pl.when(more)
        def _():
            start_spread(t + 2)
            finish_spread(t + 2)
            send_halo(t + 2)

        total = sum_round(k, 0)
        total = sum_round(k, 1)

        @pl.when(more)
        def _():
            forward_halo(t + 2)

        for b in range(2, rounds):
            total = sum_round(k, b)
        weight[...] = inverse_factor(total)
        return carry

    lax.fori_loop(0, ITERS, sweep, 0)
    final = jnp.concatenate(
        [jnp.concatenate([share[0, b], share[1, b]], axis=0) for b in range(qb)], axis=1
    )
    out_ref[...] = jnp.dot(weight[...], final, precision=HIGHEST, preferred_element_type=F32)


def per_device(start_panel, tile_values, tile_column, tile_count):
    n_rows = lax.axis_size("rows")
    n_cols = lax.axis_size("cols")
    owned, slot_dev, width, _ = tile_values.shape
    modes_all, states = start_panel.shape
    modes = modes_all // 2
    hb = owned // 2
    qb = owned // 4
    slot_ids = lax.axis_index("cols") * slot_dev + jnp.arange(slot_dev, dtype=jnp.int32)
    anchor = (lax.axis_index("rows") - 1) * owned
    index = jnp.where(slot_ids[None, :] < tile_count[:, None], tile_column - anchor, 3 * owned)
    index = jnp.pad(index, ((0, 0), (0, 128 - slot_dev)))
    rounds = 2 + int(math.log2(n_rows))
    applies = 2 * ITERS
    vmem = pltpu.VMEM
    dma = pltpu.SemaphoreType.DMA
    anywhere = pl.BlockSpec(memory_space=pl.ANY)
    in_vmem = pl.BlockSpec(memory_space=pltpu.VMEM)
    panel = pl.pallas_call(
        functools.partial(kernel, n_rows),
        out_shape=jax.ShapeDtypeStruct((modes_all, states), F32),
        in_specs=[in_vmem, anywhere, in_vmem],
        out_specs=in_vmem,
        scratch_shapes=[
            vmem((applies, 3 * owned, modes, width), F32),
            vmem((3 * owned + 1, 2 * modes, width), BF16),
            vmem((owned, modes, width), F32),
            vmem((applies, hb, modes, width), F32),
            vmem((ITERS, hb, modes, width), F32),
            vmem((2, qb, modes, width), F32),
            vmem((ITERS, qb, modes, width), F32),
            vmem((owned, slot_dev, width, width), F32),
            vmem((owned, slot_dev, width, width), F32),
            vmem((owned, width, 2 * slot_dev * width), BF16),
            vmem((owned, width, 2 * slot_dev * width), BF16),
            vmem((owned, 128), jnp.int32),
            pltpu.SMEM((owned, 128), jnp.int32),
            pltpu.SMEM((owned, 128), jnp.int32),
            vmem((modes_all, modes_all), F32),
            vmem((ITERS, rounds, modes_all, modes_all), F32),
            vmem((ITERS, rounds, modes_all, modes_all), F32),
            dma((applies, KINDS)),
            dma((applies, KINDS)),
            dma((ITERS, rounds)),
            dma((ITERS, rounds)),
            dma((4,)),
            dma((4,)),
            dma((4,)),
            dma((4,)),
        ],
        compiler_params=pltpu.CompilerParams(
            collective_id=0, has_side_effects=True, vmem_limit_bytes=50 * 1024 * 1024
        ),
        name="subspace_sweeps",
    )(start_panel, tile_values, index)
    scaling = math.sqrt(n_rows * n_cols * states)
    return panel * jnp.float32(scaling)


def solution(mesh):
    in_specs = (
        P(None, ("rows", "cols")),
        P("rows", "cols", None, None),
        P("rows", "cols"),
        P("rows"),
    )
    out_specs = P(None, ("rows", "cols"))
    return jax.shard_map(
        per_device, mesh=mesh, in_specs=in_specs, out_specs=out_specs, check_vma=False
    )
```

time: 584 us -> 161 us (0.28)
  waiting for transfers between devices: 260 us -> 0 us
  blocking collectives: 165 us -> 0 us
  Pallas kernels: 0 us -> 158 us
  matrix products: 52.7 us -> 0 us
  other arithmetic: 38.8 us -> 1.4 us
  starting transfers between devices: 35.4 us -> 0 us
  local copies, waits for them, and re-layouts: 17.7 us -> 1.67 us
  between operations: 13.8 us -> 0.02 us
    pallas_call x0 -> x1, Pallas kernels: none -> 158 us  [per_device(): pl.pallas_call(functools.partial(kernel, n_rows), out_shape=jax.ShapeDtyp...]
    reduce_scatter x6 -> x0, waiting for transfers between devices: 133 us -> none  [reduce_share(): lax.psum_scatter(partial_terms, 'cols', scatter_dimension=1, tiled=True)]
    ppermute x12 -> x0, waiting for transfers between devices: 126 us -> none  [the longest x6 66.9 us: with_halo(): lax.ppermute(lax.slice_in_dim(block, block.shape[dim] - width, None, axis...]
    psum x3 -> x0, blocking collectives: 119 us -> none  [per_device(): lower_factor = jnp.linalg.cholesky(lax.psum(local_gram, ('rows', 'cols')))]
    dot_general x9 -> x0, matrix products: 48.3 us -> none  [the longest x6 44.6 us: local_product(): jnp.einsum('disk,isnk->din', picked, tile_values, precision=lax.Precision...]
    all_gather x6 -> x0, blocking collectives: 45.6 us -> none  [fetch_owner(): return lax.all_gather(panel_part, 'cols', axis=1, tiled=True)]
    another operation x15 -> x0, other arithmetic: 36.2 us -> none  [the longest x9 19.6 us: per_device(): lower_factor = jnp.linalg.cholesky(lax.psum(local_gram, ('rows', 'cols')))]
    ppermute x12 -> x0, starting transfers between devices: 35.2 us -> none  [the longest x6 27.5 us: with_halo(): lax.ppermute(lax.slice_in_dim(block, block.shape[dim] - width, None, axis...]
  transfers between devices with their start and end apart: 18 -> 0, of which waited for: 18 -> 0; matrix products, arithmetic and copies ran while one was open for 0% -> 0% of each run, Pallas kernels for 0% -> 0%
where the time goes in v1:
time: 161 us
  Pallas kernels  158 us (98%)
  local copies, waits for them, and re-layouts  1.67 us (1%)
    pallas_call x1, Pallas kernels, per_device(): pl.pallas_call(functools.partial(kernel, n_rows), out_shape=jax.ShapeDtyp...  158 us

profile of v1, /device:TPU:0, one launch (start us, length us, event | category | flops | bytes accessed | tf_op | source)
XLA Modules:
  0.0 161.1 jit_solution(17390152310513837005)
XLA Ops:
  0.0 0.8 copy.5
  0.8 0.7 subtract_select_fusion
  1.5 0.0 copy-start
  1.5 0.9 copy-done
  2.4 158.0 %subspace_sweeps.1 = f32[64,512]{1,0:T(8,128)S(1)} custom-call(f32[64,512]{1,0:T(8,128)S(1)} %copy-done, f32[16,4,128,128]{3,2,1,0:T(8,128)} %tiles_ref.1, s32[16,128]{1,0:T(8,128)S(1)} %pad.4.slots_ref), custom_call_target="tpu_custom_call" | custom-call | tf_op jit(solution)/shard_map/subspace_sweeps/pallas_call | solution.py:357
  160.4 0.7 broadcast_multiply_fusion
  (2 shorter events, 0.0 us)
Async XLA Ops:
  1.5 0.9 copy-start

commit v2 on v1

--- a/solution.py
+++ b/solution.py
@@ -15,6 +15,17 @@
 
 GATHER, LOW, HIGH, LOW_X, HIGH_X, REDUCE, SPREAD, PAIR = range(8)
 KINDS = 8
+CHUNKS = 4
+ROW_BITS = 3
+
+
+def gram_masks(n_rows):
+    stages = [("cols", (1, 2, 3))]
+    bits = int(math.log2(n_rows))
+    for low in range(0, bits, ROW_BITS):
+        count = min(ROW_BITS, bits - low)
+        stages.append(("rows", tuple(m << low for m in range(1, 1 << count))))
+    return stages
 
 
 def inverse_factor(gram):
@@ -37,7 +48,7 @@
 def kernel(
     n_rows, start_ref, tiles_ref, slots_ref, out_ref,
     ext, planes, part, reduced, summed, share, pair, own_tiles, mate_tiles, t_hi, t_lo,
-    mate_slots, own_index, mate_index, weight, gram_send, gram_recv,
+    mate_slots, own_index, mate_index, weight, gram_total, gram_send, gram_recv,
     send_sem, recv_sem, gram_send_sem, gram_recv_sem, tile_sem, tile_send_sem, tile_recv_sem,
     slot_sem,
 ):
@@ -53,15 +64,18 @@
     width = part.shape[2]
     other_half = c + 2 - 4 * half
     mate = c + 1 - 2 * mode
-    row_rounds = int(math.log2(n_rows))
-
-    def xor_rows(b):
-        step = 1 << b
-        bit = (r // step) % 2
-        return r + step - 2 * step * bit
-
-    gram_partners = [{"cols": mate}, {"cols": other_half}]
-    gram_partners += [{"rows": xor_rows(b)} for b in range(row_rounds)]
+    def flipped(value, mask):
+        for b in range(mask.bit_length()):
+            if mask >> b & 1:
+                step = 1 << b
+                value = value + step - 2 * step * ((value // step) % 2)
+        return value
+
+    gram_stages = [
+        [{axis: flipped(r if axis == "rows" else c, mask)} for mask in masks]
+        for axis, masks in gram_masks(n_rows)
+    ]
+    gram_partners = [partner for stage in gram_stages for partner in stage]
 
     barrier = pltpu.get_barrier_semaphore()
     for partner in gram_partners:
@@ -80,32 +94,49 @@
     edges = jnp.where(r == 0, 1, 0) + jnp.where(r == n_rows - 1, 1, 0)
     pl.semaphore_wait(barrier, len(gram_partners) + 2 - edges)
 
-    def remote(src, dst, t, kind, device):
+    def remote(src, dst, t, kind, device, j=0):
         return pltpu.make_async_remote_copy(
-            src_ref=src, dst_ref=dst, send_sem=send_sem.at[t, kind], recv_sem=recv_sem.at[t, kind],
+            src_ref=src, dst_ref=dst, send_sem=send_sem.at[t, kind, j], recv_sem=recv_sem.at[t, kind, j],
             device_id=device, device_id_type=pl.DeviceIdType.MESH,
         )
 
-    def span(t, owner, piece_half):
-        return ext.at[t, pl.ds(owner * owned + piece_half * hb, hb)]
-
-    def gather_copy(t):
-        return remote(span(t, 1, half), span(t, 1, half), t, GATHER, {"cols": other_half})
-
-    def up_copy(t):
-        return remote(span(t, 1, half), span(t, 0, half), t, LOW, {"rows": r + 1})
-
-    def down_copy(t):
-        return remote(span(t, 1, half), span(t, 2, half), t, HIGH, {"rows": r - 1})
-
-    def low_forward(t):
-        return remote(span(t, 0, half), span(t, 0, half), t, LOW_X, {"cols": other_half})
-
-    def high_forward(t):
-        return remote(span(t, 2, half), span(t, 2, half), t, HIGH_X, {"cols": other_half})
-
-    def reduce_copy(t):
-        return remote(part.at[pl.ds((1 - half) * hb, hb)], reduced.at[t], t, REDUCE, {"cols": other_half})
+    cb = hb // CHUNKS
+    up, down, across = {"rows": r + 1}, {"rows": r - 1}, {"cols": other_half}
+
+    def span(t, owner, piece_half, j):
+        return ext.at[t, pl.ds(owner * owned + piece_half * hb + j * cb, cb)]
+
+    def relayed(j):
+        return j % 2 == 0
+
+    def gather_copy(t, j):
+        return remote(span(t, 1, half, j), span(t, 1, half, j), t, GATHER, across, j)
+
+    def up_copy(t, j):
+        return remote(span(t, 1, half, j), span(t, 0, half, j), t, LOW, up, j)
+
+    def down_copy(t, j):
+        return remote(span(t, 1, half, j), span(t, 2, half, j), t, HIGH, down, j)
+
+    def relay_up(t, j):
+        return remote(span(t, 1, 1 - half, j), span(t, 0, 1 - half, j), t, LOW_X, up, j)
+
+    def relay_down(t, j):
+        return remote(span(t, 1, 1 - half, j), span(t, 2, 1 - half, j), t, HIGH_X, down, j)
+
+    def low_forward(t, j):
+        return remote(span(t, 0, half, j), span(t, 0, half, j), t, LOW_X, across, j)
+
+    def high_forward(t, j):
+        return remote(span(t, 2, half, j), span(t, 2, half, j), t, HIGH_X, across, j)
+
+    def reduce_copy(t, j):
+        src = part.at[pl.ds((1 - half) * hb + j * cb, cb)]
+        return remote(src, reduced.at[t, pl.ds(j * cb, cb)], t, REDUCE, across, j)
+
+    def pair_copy(k):
+        src = summed.at[k, pl.ds((1 - mode) * qb, qb)]
+        return remote(src, pair.at[k], 2 * k + 1, PAIR, {"cols": mate})
 
     def spread_copy(t):
         place = ext.at[t, pl.ds(owned + half * hb + mode * qb, qb)]
@@ -115,40 +146,56 @@
         src = summed.at[k, pl.ds((1 - mode) * qb, qb)]
         return remote(src, pair.at[k], 2 * k + 1, PAIR, {"cols": mate})
 
+    def send_chunk(t, j):
+        gather_copy(t, j).start()
+
+        @pl.when(has_high)
+        def _():
+            up_copy(t, j).start()
+
+        @pl.when(has_low)
+        def _():
+            down_copy(t, j).start()
+
     def send_halo(t):
-        @pl.when(has_high)
-        def _():
-            up_copy(t).start()
-
-        @pl.when(has_low)
-        def _():
-            down_copy(t).start()
-
-        gather_copy(t).start()
-
-    def forward_halo(t):
-        @pl.when(has_low)
-        def _():
-            up_copy(t).wait_recv()
-            low_forward(t).start()
-
-        @pl.when(has_high)
-        def _():
-            down_copy(t).wait_recv()
-            high_forward(t).start()
+        for j in range(CHUNKS):
+            send_chunk(t, j)
+
+    def pass_halo(t):
+        for j in range(CHUNKS):
+            gather_copy(t, j).wait_recv()
+
+            @pl.when(has_high)
+            def _():
+                if relayed(j):
+                    relay_up(t, j).start()
+                down_copy(t, j).wait_recv()
+                if not relayed(j):
+                    high_forward(t, j).start()
+
+            @pl.when(has_low)
+            def _():
+                if relayed(j):
+                    relay_down(t, j).start()
+                up_copy(t, j).wait_recv()
+                if not relayed(j):
+                    low_forward(t, j).start()
 
     def finish_halo(t):
-        gather_copy(t).wait()
-
-        @pl.when(has_low)
-        def _():
-            low_forward(t).wait()
-            down_copy(t).wait_send()
-
-        @pl.when(has_high)
-        def _():
-            high_forward(t).wait()
-            up_copy(t).wait_send()
+        for j in range(CHUNKS):
+            gather_copy(t, j).wait_send()
+
+            @pl.when(has_low)
+            def _():
+                down_copy(t, j).wait_send()
+                low_forward(t, j).wait_recv()
+                (relay_down if relayed(j) else low_forward)(t, j).wait_send()
+
+            @pl.when(has_high)
+            def _():
+                up_copy(t, j).wait_send()
+                high_forward(t, j).wait_recv()
+                (relay_up if relayed(j) else high_forward)(t, j).wait_send()
 
     def start_spread(t):
         spread_copy(t).start()
@@ -209,7 +256,6 @@
     for q in range(tile_parts):
         tile_local(q).wait()
         split_tiles(own_tiles, q, 0)
-    forward_halo(0)
     for q in range(tile_parts):
         tile_remote(q).wait()
         split_tiles(mate_tiles, q, slot_dev)
@@ -239,58 +285,91 @@
 
         lax.fori_loop(0, blocks, convert, 0, unroll=4)
 
-        def product(i, carry):
-            row_product((1 - half) * hb + i)
-            return carry
-
-        lax.fori_loop(0, hb, product, 0, unroll=2)
-        reduce_copy(t).start()
-
-        def product_own(i, carry):
-            row_product(half * hb + i)
-            return carry
-
-        lax.fori_loop(0, hb, product_own, 0, unroll=2)
-        reduce_copy(t).wait()
-
-    def add_reduced(t, target):
-        def body(b, carry):
-            ext[target, owned + half * hb + b] = part[half * hb + b] + reduced[t, b]
-            return carry
-
-        lax.fori_loop(0, hb, body, 0)
-
-    def gram_round(k, b):
-        copy = pltpu.make_async_remote_copy(
-            src_ref=gram_send.at[k, b], dst_ref=gram_recv.at[k, b], send_sem=gram_send_sem.at[k, b],
-            recv_sem=gram_recv_sem.at[k, b], device_id=gram_partners[b], device_id_type=pl.DeviceIdType.MESH,
+        for first in (1 - half, half):
+            for j in range(CHUNKS):
+                def product(i, carry):
+                    row_product(first * hb + j * cb + i)
+                    return carry
+
+                lax.fori_loop(0, cb, product, 0, unroll=True)
+                if first is not half:
+                    reduce_copy(t, j).start()
+
+    def reduce_chunk(t, j):
+        reduce_copy(t, j).wait_recv()
+        return [(j * cb + b, part[half * hb + j * cb + b] + reduced[t, j * cb + b]) for b in range(cb)]
+
+    def finish_reduce(t):
+        for j in range(CHUNKS):
+            reduce_copy(t, j).wait_send()
+
+    offsets = [0]
+    for stage in gram_stages:
+        offsets.append(offsets[-1] + len(stage))
+
+    def gram_copy(k, stage, p):
+        slot = offsets[stage] + p
+        return pltpu.make_async_remote_copy(
+            src_ref=gram_send.at[k, stage], dst_ref=gram_recv.at[k, slot], send_sem=gram_send_sem.at[k, slot],
+            recv_sem=gram_recv_sem.at[k, slot], device_id=gram_stages[stage][p],
+            device_id_type=pl.DeviceIdType.MESH,
         )
-        return copy
-
-    rounds = len(gram_partners)
-
-    def sum_round(k, b):
-        gram_round(k, b).wait()
-        total = gram_send[k, b] + gram_recv[k, b]
-        if b + 1 < rounds:
-            gram_send[k, b + 1] = total
-            gram_round(k, b + 1).start()
-        return total
+
+    def start_stage(k, stage, value):
+        gram_send[k, stage] = value
+        for p in range(len(gram_stages[stage])):
+            gram_copy(k, stage, p).start()
+
+    def end_stage(k, stage):
+        terms = [gram_send[k, stage]]
+        for p in range(len(gram_stages[stage])):
+            gram_copy(k, stage, p).wait()
+            terms.append(gram_recv[k, offsets[stage] + p])
+        while len(terms) > 1:
+            terms = [terms[p] + terms[p + 1] for p in range(0, len(terms), 2)]
+        if stage + 1 < len(gram_stages):
+            start_stage(k, stage + 1, terms[0])
+        else:
+            gram_total[...] = terms[0]
+
+    def factor(k):
+        for stage in range(2, len(gram_stages)):
+            end_stage(k, stage)
+        weight[...] = inverse_factor(gram_total[...])
 
     def sweep(k, carry):
         t = 2 * k
+        later = k > 0
+        pass_halo(t)
+
+        @pl.when(later)
+        def _():
+            end_stage(k - 1, 0)
+
         finish_halo(t)
         apply(t)
-        add_reduced(t, t + 1)
-        send_halo(t + 1)
-        forward_halo(t + 1)
+
+        @pl.when(later)
+        def _():
+            end_stage(k - 1, 1)
+
+        for j in range(CHUNKS):
+            for b, value in reduce_chunk(t, j):
+                ext[t + 1, owned + half * hb + b] = value
+            send_chunk(t + 1, j)
+        finish_reduce(t)
+        pass_halo(t + 1)
+
+        @pl.when(later)
+        def _():
+            factor(k - 1)
+
         finish_halo(t + 1)
         apply(t + 1)
-        def close(b, carry):
-            summed[k, b] = part[half * hb + b] + reduced[t + 1, b]
-            return carry
-
-        lax.fori_loop(0, hb, close, 0)
+        for j in range(CHUNKS):
+            for b, value in reduce_chunk(t + 1, j):
+                summed[k, b] = value
+        finish_reduce(t + 1)
         pair_copy(k).start()
         for b in range(qb):
             share[mode, b] = summed[k, mode * qb + b]
@@ -304,32 +383,23 @@
         for b in range(qb):
             for h in range(2):
                 share[h, b] = mixed[h * modes : (h + 1) * modes, b * width : (b + 1) * width]
-        gram_send[k, 0] = lax.dot_general(
+        gram = lax.dot_general(
             mixed, mixed, (((1,), (1,)), ((), ())), precision=HIGHEST, preferred_element_type=F32
         )
-        gram_round(k, 0).start()
-
-        more = k < ITERS - 1
-
-        @pl.when(more)
+        start_stage(k, 0, gram)
+
+        @pl.when(k < ITERS - 1)
         def _():
             start_spread(t + 2)
             finish_spread(t + 2)
             send_halo(t + 2)
 
-        total = sum_round(k, 0)
-        total = sum_round(k, 1)
-
-        @pl.when(more)
-        def _():
-            forward_halo(t + 2)
-
-        for b in range(2, rounds):
-            total = sum_round(k, b)
-        weight[...] = inverse_factor(total)
         return carry
 
     lax.fori_loop(0, ITERS, sweep, 0)
+    end_stage(ITERS - 1, 0)
+    end_stage(ITERS - 1, 1)
+    factor(ITERS - 1)
     final = jnp.concatenate(
         [jnp.concatenate([share[0, b], share[1, b]], axis=0) for b in range(qb)], axis=1
     )
@@ -348,7 +418,8 @@
     anchor = (lax.axis_index("rows") - 1) * owned
     index = jnp.where(slot_ids[None, :] < tile_count[:, None], tile_column - anchor, 3 * owned)
     index = jnp.pad(index, ((0, 0), (0, 128 - slot_dev)))
-    rounds = 2 + int(math.log2(n_rows))
+    stages = gram_masks(n_rows)
+    peers = sum(len(masks) for _, masks in stages)
     applies = 2 * ITERS
     vmem = pltpu.VMEM
     dma = pltpu.SemaphoreType.DMA
@@ -375,12 +446,13 @@
             pltpu.SMEM((owned, 128), jnp.int32),
             pltpu.SMEM((owned, 128), jnp.int32),
             vmem((modes_all, modes_all), F32),
-            vmem((ITERS, rounds, modes_all, modes_all), F32),
-            vmem((ITERS, rounds, modes_all, modes_all), F32),
-            dma((applies, KINDS)),
-            dma((applies, KINDS)),
-            dma((ITERS, rounds)),
-            dma((ITERS, rounds)),
+            vmem((modes_all, modes_all), F32),
+            vmem((ITERS, len(stages), modes_all, modes_all), F32),
+            vmem((ITERS, peers, modes_all, modes_all), F32),
+            dma((applies, KINDS, CHUNKS)),
+            dma((applies, KINDS, CHUNKS)),
+            dma((ITERS, peers)),
+            dma((ITERS, peers)),
             dma((4,)),
             dma((4,)),
             dma((4,)),

time: 161 us -> 138 us (0.86)
  Pallas kernels: 158 us -> 135 us
    pallas_call x1, Pallas kernels: 158 us -> 135 us  [per_device(): pl.pallas_call(functools.partial(kernel, n_rows), out_shape=jax.ShapeDtyp...]
where the time goes in v2:
time: 138 us
  Pallas kernels  135 us (98%)
  local copies, waits for them, and re-layouts  1.67 us (1%)
  other arithmetic  1.4 us (1%)
    pallas_call x1, Pallas kernels, per_device(): pl.pallas_call(functools.partial(kernel, n_rows), out_shape=jax.ShapeDtyp...  135 us

profile of v2, /device:TPU:0, one launch (start us, length us, event | category | flops | bytes accessed | tf_op | source)
XLA Modules:
  0.0 138.3 jit_solution(2666386707820257944)
XLA Ops:
  0.0 0.8 copy.5
  0.8 0.7 subtract_select_fusion
  1.5 0.0 copy-start
  1.5 0.9 copy-done
  2.4 135.3 %subspace_sweeps.1 = f32[64,512]{1,0:T(8,128)S(1)} custom-call(f32[64,512]{1,0:T(8,128)S(1)} %copy-done, f32[16,4,128,128]{3,2,1,0:T(8,128)} %tiles_ref.1, s32[16,128]{1,0:T(8,128)S(1)} %pad.4.slots_ref), custom_call_target="tpu_custom_call" | custom-call | tf_op jit(solution)/shard_map/subspace_sweeps/pallas_call | solution.py:428
  137.7 0.7 broadcast_multiply_fusion
  (2 shorter events, 0.0 us)
Async XLA Ops:
  1.5 0.9 copy-start

commit v3 on v2

--- a/solution.py
+++ b/solution.py
@@ -39,7 +39,7 @@
         column = both[:, j : j + 1]
         row = both[j : j + 1, :]
         pivot = both[j : j + 1, j : j + 1]
-        factor = jnp.where(row_ids > j, column / pivot, 0.0)
+        factor = jnp.where(row_ids > j, column, 0.0) * (1.0 / pivot)
         scale = jnp.where(row_ids == j, lax.rsqrt(pivot), scale)
         both = both - factor * row
     return both[:, size:] * scale
@@ -107,7 +107,7 @@
         return ext.at[t, pl.ds(owner * owned + piece_half * hb + j * cb, cb)]
 
     def relayed(j):
-        return j % 2 == 0
+        return False
 
     def gather_copy(t, j):
         return remote(span(t, 1, half, j), span(t, 1, half, j), t, GATHER, across, j)
@@ -163,7 +163,8 @@
 
     def pass_halo(t):
         for j in range(CHUNKS):
-            gather_copy(t, j).wait_recv()
+            if relayed(j):
+                gather_copy(t, j).wait_recv()
 
             @pl.when(has_high)
             def _():
@@ -184,6 +185,8 @@
     def finish_halo(t):
         for j in range(CHUNKS):
             gather_copy(t, j).wait_send()
+            if not relayed(j):
+                gather_copy(t, j).wait_recv()
 
             @pl.when(has_low)
             def _():
@@ -256,6 +259,7 @@
     for q in range(tile_parts):
         tile_local(q).wait()
         split_tiles(own_tiles, q, 0)
+    pass_halo(0)
     for q in range(tile_parts):
         tile_remote(q).wait()
         split_tiles(mate_tiles, q, slot_dev)
@@ -340,7 +344,6 @@
     def sweep(k, carry):
         t = 2 * k
         later = k > 0
-        pass_halo(t)
 
         @pl.when(later)
         def _():
@@ -383,16 +386,22 @@
         for b in range(qb):
             for h in range(2):
                 share[h, b] = mixed[h * modes : (h + 1) * modes, b * width : (b + 1) * width]
+        more = k < ITERS - 1
+
+        @pl.when(more)
+        def _():
+            start_spread(t + 2)
+
         gram = lax.dot_general(
             mixed, mixed, (((1,), (1,)), ((), ())), precision=HIGHEST, preferred_element_type=F32
         )
         start_stage(k, 0, gram)
 
-        @pl.when(k < ITERS - 1)
-        def _():
-            start_spread(t + 2)
+        @pl.when(more)
+        def _():
             finish_spread(t + 2)
             send_halo(t + 2)
+            pass_halo(t + 2)
 
         return carry
 

time: 138 us -> 134 us (0.971)
  Pallas kernels: 135 us -> 131 us
    pallas_call x1, Pallas kernels: 135 us -> 131 us  [per_device(): pl.pallas_call(functools.partial(kernel, n_rows), out_shape=jax.ShapeDtyp...]
where the time goes in v3:
time: 134 us
  Pallas kernels  131 us (98%)
  local copies, waits for them, and re-layouts  1.67 us (1%)
  other arithmetic  1.4 us (1%)
    pallas_call x1, Pallas kernels, per_device(): pl.pallas_call(functools.partial(kernel, n_rows), out_shape=jax.ShapeDtyp...  131 us

profile of v3, /device:TPU:0, one launch (start us, length us, event | category | flops | bytes accessed | tf_op | source)
XLA Modules:
  0.0 134.1 jit_solution(2668178449052354102)
XLA Ops:
  0.0 0.8 copy.5
  0.8 0.7 subtract_select_fusion
  1.5 0.0 copy-start
  1.5 0.9 copy-done
  2.4 131.0 %subspace_sweeps.1 = f32[64,512]{1,0:T(8,128)S(1)} custom-call(f32[64,512]{1,0:T(8,128)S(1)} %copy-done, f32[16,4,128,128]{3,2,1,0:T(8,128)} %tiles_ref.1, s32[16,128]{1,0:T(8,128)S(1)} %pad.4.slots_ref), custom_call_target="tpu_custom_call" | custom-call | tf_op jit(solution)/shard_map/subspace_sweeps/pallas_call | solution.py:437
  133.5 0.7 broadcast_multiply_fusion
  (2 shorter events, 0.0 us)
Async XLA Ops:
  1.5 0.9 copy-start
